TPU v7x, 128 devices: a whole 4x4x4 slice. The times are simulated.
128 devices in a mesh: row: 8 (over z_lo, y), col: 16 (over z_hi, x, core).
Axes of the slice: x: 4, y: 4, z: 4 (z_hi: 2, z_lo: 2; z = z_hi * 2 + z_lo), core: 2. Of those that a mesh axis runs over, the one named last changes fastest.
Arguments:
- observed: float32 [4, 65536], P(None, ('row', 'col')), may hold values from -50 to 50
- tile_values: bfloat16 [256, 32, 256, 256], P('row', 'col'), may hold values from -2.2649514 to 2.2649514
- tile_cols: int32 [256, 32], P('row', 'col'), may hold values from 0 to 255
Outputs:
- solution: float32 [4, 1048576], P(None, ('col', 'row'))
- residual_ratio: float32 [4], replicated
All inputs are finite; a program needn't handle non-finite values.
Results may differ from a plain program's by a relative error of at most 0.0021.
Values may be sent and summed in bfloat16 or wider, within the bound.
A program may use at most 128 MiB of HBM per device.

v0:
```python
import jax
import jax.numpy as jnp
from jax import lax
from jax.sharding import PartitionSpec as P

ITERS = 2
N = 1048576
epsilon_sq = 1e-06


def local(observed, tile_values, tile_cols):
    right_sides = observed.shape[0]
    row_tiles = tile_values.shape[0]
    per_block = tile_values.shape[1]
    tile_size = tile_values.shape[2]
    col_tiles = N // (tile_size * lax.axis_size("col"))
    panel_len = col_tiles * tile_size
    share_len = panel_len // lax.axis_size("row")
    flat_cols = tile_cols.reshape(-1)

    def adjoint_map(left_bf):
        gathered = lax.all_gather(left_bf, "col", axis=1, tiled=True).reshape(
            right_sides, row_tiles, tile_size
        )
        tile_terms = jnp.einsum(
            "rktj,nrt->nrkj", tile_values, gathered, preferred_element_type=jnp.float32
        )
        tile_terms = tile_terms.reshape(right_sides, row_tiles * per_block, tile_size)
        placed = (
            jnp.zeros((right_sides, col_tiles, tile_size), jnp.float32)
            .at[:, flat_cols]
            .add(tile_terms)
        )
        placed = placed.reshape(right_sides, panel_len)
        summed = lax.psum_scatter(placed, "row", scatter_dimension=1, tiled=True)
        return summed

    def lanczos_pair(left_raw, right_vec):
        beta_sq = lax.psum(jnp.sum(left_raw * left_raw, axis=1), ("row", "col"))
        beta_norm = jnp.sqrt(beta_sq + epsilon_sq)
        product = adjoint_map(left_raw.astype(jnp.bfloat16))
        right_raw = product / beta_norm[:, None] - beta_norm[:, None] * right_vec
        alpha_sq = lax.psum(jnp.sum(right_raw * right_raw, axis=1), ("row", "col"))
        alpha_norm = jnp.sqrt(alpha_sq + epsilon_sq)
        return (beta_norm, alpha_norm, right_raw)

    blank_right = jnp.zeros((right_sides, share_len), jnp.float32)
    beta_norm, alpha_norm, right_raw = lanczos_pair(observed, blank_right)
    first_beta = beta_norm
    left_vec = observed / beta_norm[:, None]
    right_vec = right_raw / alpha_norm[:, None]
    right_bf = right_raw.astype(jnp.bfloat16)
    phibar = beta_norm
    rhobar = alpha_norm
    direction = right_vec
    solution = jnp.zeros_like(right_vec)
    for iteration in range(ITERS):
        whole_panel = lax.all_gather(right_bf, "row", axis=1, tiled=True)
        picked = jnp.take(whole_panel.reshape(right_sides, col_tiles, tile_size), tile_cols, axis=1)
        partial_rows = jnp.einsum(
            "rktj,nrkj->nrt", tile_values, picked, preferred_element_type=jnp.float32
        )
        left_raw = (
            lax.psum_scatter(
                partial_rows.reshape(right_sides, row_tiles * tile_size),
                "col",
                scatter_dimension=1,
                tiled=True,
            )
            / alpha_norm[:, None]
            - alpha_norm[:, None] * left_vec
        )
        beta_norm, alpha_norm, right_raw = lanczos_pair(left_raw, right_vec)
        left_vec = left_raw / beta_norm[:, None]
        right_vec = right_raw / alpha_norm[:, None]
        right_bf = right_raw.astype(jnp.bfloat16)
        rho_val = jnp.sqrt(rhobar * rhobar + beta_norm * beta_norm)
        cosine = rhobar / rho_val
        sine_val = beta_norm / rho_val
        theta_val = sine_val * alpha_norm
        rhobar = -cosine * alpha_norm
        phi_val = cosine * phibar
        phibar = sine_val * phibar
        solution = solution + (phi_val / rho_val)[:, None] * direction
        direction = right_vec - (theta_val / rho_val)[:, None] * direction
    return (solution, phibar / first_beta)


def solution(mesh):
    in_specs = (P(None, ("row", "col")), P("row", "col", None, None), P("row", "col"))
    out_specs = (P(None, ("col", "row")), P())
    return jax.shard_map(local, mesh=mesh, in_specs=in_specs, out_specs=out_specs, check_vma=False)
```

profile of v0, /device:TPU:1, one launch (start us, length us, event | category | flops | bytes accessed | tf_op | source)
XLA Modules:
  0.0 1160.2 jit_solution(9524676217768432283)
XLA Ops:
  7.2 0.0 reduce-scatter.13.cloned.1.call-start
  7.2 0.9 fusion.20
  8.1 26.5 %all_gather.12 = bf16[4,8192]{1,0:T(4,128)(2,1)S(1)} all-gather(bf16[4,512]{1,0:T(4,128)(2,1)S(1)} %get-tuple-element.13), channel_id=1, replica_groups=mesh['row'=8,'col'=16] {'col'}, dimensions={1}, use_global_device_ids=true | all-gather | bytes 69632 | tf_op jit(solution)/shard_map/all_gather | solution.py:22
  34.6 0.8 copy.17
  35.4 0.1 reshape.77
  35.5 4.6 fusion.21
  40.0 0.1 broadcast.38.clone
  40.2 2.8 scatter_fusion
  43.0 16.1 %copy.26 = f32[4,65536]{0,1:T(8,128)} copy(f32[4,65536]{1,0:T(4,128)S(1)} %bitcast.65) | data formatting | bytes 2097152
  59.1 0.0 copy-start.1
  59.1 0.0 reduce-scatter.13.cloned.1.call-update
  59.1 0.0 reduce-scatter.15.cloned.1.call-start
  59.2 369.9 %psum.35 = f32[4]{0:T(128)S(1)} all-reduce(f32[4]{0:T(128)S(1)} %get-tuple-element.14), channel_id=1, replica_groups=mesh['row'=8,'col'=16] {'row','col'}, use_global_device_ids=true, to_apply=%region_3.0 | all-reduce | flops 4 | bytes 32 | tf_op jit(solution)/shard_map/psum | solution.py:39
  429.1 0.0 copy-done.1
  429.1 0.1 copy.19
  429.2 0.1 reshape.124
  429.3 0.1 copy.18
  429.4 0.0 reduce-scatter.13.cloned.1.call-done
  429.5 2.8 copy.27
  432.3 0.3 multiply_reduce_fusion.1
  432.6 22.8 %all_gather.13 = bf16[4,65536]{1,0:T(4,128)(2,1)S(1)} all-gather(bf16[4,8192]{1,0:T(4,128)(2,1)S(1)} %convert_element_type.13), channel_id=1, replica_groups=mesh['row'=8,'col'=16] {'row'}, dimensions={1}, use_global_device_ids=true | all-gather | bytes 589824 | tf_op jit(solution)/shard_map/all_gather | solution.py:58
  455.4 0.7 gather_fusion
  456.1 0.0 copy-start
  456.1 5.7 fusion.2
  461.8 2.6 copy.28
  464.4 0.0 reduce-scatter.15.cloned.1.call-update
  464.5 0.0 reduce-scatter.17.cloned.1.call-start
  464.5 74.8 %psum.36 = f32[4]{0:T(128)S(1)} all-reduce(f32[4]{0:T(128)S(1)} %get-tuple-element.11), channel_id=1, replica_groups=mesh['row'=8,'col'=16] {'row','col'}, use_global_device_ids=true, to_apply=%region_5.0 | all-reduce | flops 4 | bytes 32 | tf_op jit(solution)/shard_map/psum | solution.py:43
  539.4 8.0 reduce-scatter.15.cloned.1.call-done
  547.4 1.1 copy.29
  548.4 0.0 copy-done
  548.4 0.2 multiply_reduce_fusion.2
  548.7 23.2 %all_gather.14 = bf16[4,8192]{1,0:T(4,128)(2,1)S(1)} all-gather(bf16[4,512]{1,0:T(4,128)(2,1)S(1)} %convert_element_type.14), channel_id=1, replica_groups=mesh['row'=8,'col'=16] {'col'}, dimensions={1}, use_global_device_ids=true | all-gather | bytes 69632 | tf_op jit(solution)/shard_map/all_gather | solution.py:22
  571.8 4.6 fusion.22
  576.4 0.1 broadcast.38
  576.6 2.8 scatter_fusion.1
  579.4 16.1 %copy.30 = f32[4,65536]{0,1:T(8,128)} copy(f32[4,65536]{1,0:T(4,128)S(1)} %bitcast.64) | data formatting | bytes 2097152
  595.5 0.0 reduce-scatter.17.cloned.1.call-update
  595.5 0.0 reduce-scatter.19.cloned.1.call-start
  595.6 371.7 %psum.37 = f32[4]{0:T(128)S(1)} all-reduce(f32[4]{0:T(128)S(1)} %get-tuple-element.9), channel_id=1, replica_groups=mesh['row'=8,'col'=16] {'row','col'}, use_global_device_ids=true, to_apply=%region_8.10 | all-reduce | flops 4 | bytes 32 | tf_op jit(solution)/shard_map/psum | solution.py:39
  967.3 0.0 reduce-scatter.17.cloned.1.call-done
  967.3 2.8 copy.31
  970.2 0.1 fusion.19
  970.3 23.0 %all_gather.15 = bf16[4,65536]{1,0:T(4,128)(2,1)S(1)} all-gather(bf16[4,8192]{1,0:T(4,128)(2,1)S(1)} %get-tuple-element.7), channel_id=1, replica_groups=mesh['row'=8,'col'=16] {'row'}, dimensions={1}, use_global_device_ids=true | all-gather | bytes 589824 | tf_op jit(solution)/shard_map/all_gather | solution.py:58
  993.3 0.7 gather_fusion.1
  994.0 5.7 fusion
  999.7 2.6 copy.32
  1002.3 0.2 multiply_reduce_fusion
  1002.5 0.0 reduce-scatter.19.cloned.1.call-update
  1002.5 75.0 %psum.38 = f32[4]{0:T(128)S(1)} all-reduce(f32[4]{0:T(128)S(1)} %multiply_reduce_fusion), channel_id=1, replica_groups=mesh['row'=8,'col'=16] {'row','col'}, use_global_device_ids=true, to_apply=%region_12.14 | all-reduce | flops 4 | bytes 32 | tf_op jit(solution)/shard_map/psum | solution.py:43
  1077.5 8.0 reduce-scatter.19.cloned.1.call-done
  1085.5 1.1 copy.33
  1086.5 0.2 fusion.11
  1086.7 65.6 %psum.39 = f32[4]{0:T(128)S(1)} all-reduce(f32[4]{0:T(128)S(1)} %fusion.11), channel_id=1, replica_groups=mesh['row'=8,'col'=16] {'row','col'}, use_global_device_ids=true, to_apply=%region_15.17 | all-reduce | flops 4 | bytes 32 | tf_op jit(solution)/shard_map/psum | solution.py:39
  1152.3 0.6 multiply_divide_fusion
  1152.9 0.8 multiply_add_fusion
  (11 shorter events, 0.1 us)
Async XLA Ops:
  7.2 422.3 %reduce-scatter.13.cloned.1.call-start = ((), (), s32[]{:S(2)}) async-start(), calls=%async_computation.4 | async-start | bytes 37748736
  59.1 370.0 %copy-start.1 = (s32[32,2]{0,1:T(2,128)S(1)}, s32[32,2]{0,1:T(2,128)}, u32[]{:S(2)}) copy-start(s32[32,2]{0,1:T(2,128)} %param.7) | copy-start | bytes 772
  59.1 488.2 %reduce-scatter.15.cloned.1.call-start = ((), (), s32[]{:S(2)}) async-start(), calls=%async_computation.5 | async-start | bytes 4456448
  456.1 92.3 %copy-start = (f32[4,512]{1,0:T(4,128)S(1)}, f32[4,512]{1,0:T(4,128)}, u32[]{:S(2)}) copy-start(f32[4,512]{1,0:T(4,128)} %param.5) | copy-start | bytes 24580
  464.5 502.9 %reduce-scatter.17.cloned.1.call-start = ((), (), s32[]{:S(2)}) async-start(), calls=%async_computation.6 | async-start | bytes 37748736
  595.5 490.0 %reduce-scatter.19.cloned.1.call-start = ((), (), s32[]{:S(2)}) async-start(), calls=%async_computation.7 | async-start | bytes 4456448
Sparse Core Ops, SparseCore 0:
  59.3 325.6 reduce-scatter.12
  464.6 82.7 reduce-scatter.14
  595.6 327.5 reduce-scatter.16
  1002.6 82.7 reduce-scatter.18
where the time goes:
time: 1160 us
  blocking collectives  1050 us (91%)
  local copies, waits for them, and re-layouts  48 us (4%)
  matrix products  20.5 us (2%)
  waiting for transfers between devices  16.1 us (1%)
  between operations  13.9 us (1%)
    psum x3, blocking collectives, lanczos_pair(): beta_sq = lax.psum(jnp.sum(left_raw * left_raw, axis=1), ('row', 'col'))  807 us
    psum x2, blocking collectives, lanczos_pair(): alpha_sq = lax.psum(jnp.sum(right_raw * right_raw, axis=1), ('row', 'col'))  150 us
    all_gather x2, blocking collectives, adjoint_map(): lax.all_gather(left_bf, 'col', axis=1, tiled=True)  49.7 us
    unnamed x13, local copies, waits for them, and re-layouts  46 us
    all_gather x2, blocking collectives, local(): whole_panel = lax.all_gather(right_bf, 'row', axis=1, tiled=True)  45.8 us
  transfers between devices with their start and end apart: 4, of which 2 were waited for; matrix products, arithmetic and copies ran while one was open for 0% of the time, Pallas kernels for 0%

commit v1 on v0

--- a/solution.py
+++ b/solution.py
@@ -55,7 +55,9 @@
     direction = right_vec
     solution = jnp.zeros_like(right_vec)
     for iteration in range(ITERS):
-        whole_panel = lax.all_gather(right_bf, "row", axis=1, tiled=True)
+        whole_panel = jnp.concatenate(
+            lax.all_to_all(jnp.stack([right_bf] * lax.axis_size("row")), "row", 0, 0), axis=1
+        )
         picked = jnp.take(whole_panel.reshape(right_sides, col_tiles, tile_size), tile_cols, axis=1)
         partial_rows = jnp.einsum(
             "rktj,nrkj->nrt", tile_values, picked, preferred_element_type=jnp.float32

time: 1160 us -> 1240 us (1.069)
  waiting for transfers between devices: 16.1 us -> 151 us
  blocking collectives: 1050 us -> 988 us
    unnamed x8, waiting for transfers between devices: 16.1 us -> 151 us
    all_gather x2 -> x0, blocking collectives: 45.8 us -> none  [local(): whole_panel = lax.all_gather(right_bf, 'row', axis=1, tiled=True)]
    psum x2, blocking collectives: 150 us -> 131 us  [lanczos_pair(): alpha_sq = lax.psum(jnp.sum(right_raw * right_raw, axis=1), ('row', 'col'))]
  transfers between devices with their start and end apart: 4 -> 6, of which waited for: 2 -> 2; matrix products, arithmetic and copies ran while one was open for 0% -> 0% of each run, Pallas kernels for 0% -> 0%
where the time goes in v1:
time: 1240 us
  blocking collectives  988 us (80%)
  waiting for transfers between devices  151 us (12%)
  local copies, waits for them, and re-layouts  49.9 us (4%)
  matrix products  20.5 us (2%)
  between operations  13.9 us (1%)
    psum x3, blocking collectives, lanczos_pair(): beta_sq = lax.psum(jnp.sum(left_raw * left_raw, axis=1), ('row', 'col'))  808 us
    unnamed x8, waiting for transfers between devices  151 us
    psum x2, blocking collectives, lanczos_pair(): alpha_sq = lax.psum(jnp.sum(right_raw * right_raw, axis=1), ('row', 'col'))  131 us
    all_gather x2, blocking collectives, adjoint_map(): lax.all_gather(left_bf, 'col', axis=1, tiled=True)  49.6 us
    unnamed x13, local copies, waits for them, and re-layouts  46 us
  transfers between devices with their start and end apart: 6, of which 2 were waited for; matrix products, arithmetic and copies ran while one was open for 0% of the time, Pallas kernels for 0%

profile of v1, /device:TPU:1, one launch (start us, length us, event | category | flops | bytes accessed | tf_op | source)
XLA Modules:
  0.0 1240.2 jit_solution(4951896587201468946)
XLA Ops:
  7.2 0.0 reduce-scatter.13.cloned.1.call-start
  7.2 0.9 fusion.20
  8.1 26.5 %all_gather.6 = bf16[4,8192]{1,0:T(4,128)(2,1)S(1)} all-gather(bf16[4,512]{1,0:T(4,128)(2,1)S(1)} %get-tuple-element.13), channel_id=1, replica_groups=mesh['row'=8,'col'=16] {'col'}, dimensions={1}, use_global_device_ids=true | all-gather | bytes 69632 | tf_op jit(solution)/shard_map/all_gather | solution.py:22
  34.6 0.8 copy.17
  35.4 0.1 reshape.81
  35.5 4.6 fusion.21
  40.0 0.1 broadcast.42.clone
  40.2 2.8 scatter_fusion
  43.0 16.1 %copy.30 = f32[4,65536]{0,1:T(8,128)} copy(f32[4,65536]{1,0:T(4,128)S(1)} %bitcast.69) | data formatting | bytes 2097152
  59.1 0.0 copy-start.1
  59.1 0.0 reduce-scatter.13.cloned.1.call-update
  59.1 370.0 %psum.35 = f32[4]{0:T(128)S(1)} all-reduce(f32[4]{0:T(128)S(1)} %get-tuple-element.14), channel_id=1, replica_groups=mesh['row'=8,'col'=16] {'row','col'}, use_global_device_ids=true, to_apply=%region_3.0 | all-reduce | flops 4 | bytes 32 | tf_op jit(solution)/shard_map/psum | solution.py:39
  429.1 0.0 reduce-scatter.13.cloned.1.call-done
  429.1 2.8 copy.31
  432.0 0.3 multiply_reduce_fusion.1
  432.3 0.9 stack.4
  433.2 3.5 all-to-all-start
  436.7 0.0 reduce-scatter.15.cloned.1.call-start
  436.7 0.0 copy-done.1
  436.8 0.1 copy.20
  436.9 0.1 reshape.128
  437.0 0.1 copy.18
  437.1 65.5 %psum.36 = f32[4]{0:T(128)S(1)} all-reduce(f32[4]{0:T(128)S(1)} %get-tuple-element.11), channel_id=1, replica_groups=mesh['row'=8,'col'=16] {'row','col'}, use_global_device_ids=true, to_apply=%region_5.0 | all-reduce | flops 4 | bytes 32 | tf_op jit(solution)/shard_map/psum | solution.py:43
  502.6 0.0 all-to-all-done
  502.6 0.7 gather_fusion
  503.3 0.0 copy-start
  503.3 5.7 fusion.2
  508.9 2.6 copy.32
  511.6 0.0 reduce-scatter.15.cloned.1.call-update
  511.6 0.0 reduce-scatter.17.cloned.1.call-start
  511.7 75.6 %reduce-scatter.15.cloned.1.call-done = f32[512,4]{1,0:T(8,128)} async-done(((f32[8192,4]{1,0:T(8,128)}), f32[512,4]{1,0:T(8,128)}) %reduce-scatter.15.cloned.1.call-update) | async-done | bytes 8208
  587.3 1.1 copy.33
  588.3 0.0 copy-done
  588.3 0.2 multiply_reduce_fusion.2
  588.6 23.2 %all_gather.7 = bf16[4,8192]{1,0:T(4,128)(2,1)S(1)} all-gather(bf16[4,512]{1,0:T(4,128)(2,1)S(1)} %convert_element_type.14), channel_id=1, replica_groups=mesh['row'=8,'col'=16] {'col'}, dimensions={1}, use_global_device_ids=true | all-gather | bytes 69632 | tf_op jit(solution)/shard_map/all_gather | solution.py:22
  611.7 4.6 fusion.22
  616.3 0.1 broadcast.42
  616.4 2.8 scatter_fusion.1
  619.3 16.1 %copy.34 = f32[4,65536]{0,1:T(8,128)} copy(f32[4,65536]{1,0:T(4,128)S(1)} %bitcast.68) | data formatting | bytes 2097152
  635.4 0.0 reduce-scatter.17.cloned.1.call-update
  635.4 372.0 %psum.37 = f32[4]{0:T(128)S(1)} all-reduce(f32[4]{0:T(128)S(1)} %get-tuple-element.9), channel_id=1, replica_groups=mesh['row'=8,'col'=16] {'row','col'}, use_global_device_ids=true, to_apply=%region_8.10 | all-reduce | flops 4 | bytes 32 | tf_op jit(solution)/shard_map/psum | solution.py:39
  1007.4 0.0 reduce-scatter.17.cloned.1.call-done
  1007.4 2.8 copy.35
  1010.3 0.1 fusion.19
  1010.4 0.9 stack.5
  1011.4 3.5 all-to-all-start.1
  1014.9 0.0 reduce-scatter.19.cloned.1.call-start
  1014.9 0.2 multiply_reduce_fusion
  1015.1 65.5 %psum.38 = f32[4]{0:T(128)S(1)} all-reduce(f32[4]{0:T(128)S(1)} %multiply_reduce_fusion), channel_id=1, replica_groups=mesh['row'=8,'col'=16] {'row','col'}, use_global_device_ids=true, to_apply=%region_12.14 | all-reduce | flops 4 | bytes 32 | tf_op jit(solution)/shard_map/psum | solution.py:43
  1080.6 0.0 all-to-all-done.1
  1080.6 0.7 gather_fusion.1
  1081.3 5.7 fusion
  1086.9 2.6 copy.36
  1089.6 0.0 reduce-scatter.19.cloned.1.call-update
  1089.6 75.7 %reduce-scatter.19.cloned.1.call-done = f32[512,4]{1,0:T(8,128)} async-done(((f32[8192,4]{1,0:T(8,128)}), f32[512,4]{1,0:T(8,128)}) %reduce-scatter.19.cloned.1.call-update) | async-done | bytes 8208
  1165.2 1.1 copy.37
  1166.3 0.2 fusion.11
  1166.5 65.8 %psum.39 = f32[4]{0:T(128)S(1)} all-reduce(f32[4]{0:T(128)S(1)} %fusion.11), channel_id=1, replica_groups=mesh['row'=8,'col'=16] {'row','col'}, use_global_device_ids=true, to_apply=%region_15.17 | all-reduce | flops 4 | bytes 32 | tf_op jit(solution)/shard_map/psum | solution.py:39
  1232.3 0.6 multiply_divide_fusion
  1232.9 0.8 multiply_add_fusion
  (11 shorter events, 0.1 us)
Async XLA Ops:
  7.2 421.9 %reduce-scatter.13.cloned.1.call-start = ((), (), s32[]{:S(2)}) async-start(), calls=%async_computation.6 | async-start | bytes 37748736
  59.1 377.6 %copy-start.1 = (s32[32,2]{0,1:T(2,128)S(1)}, s32[32,2]{0,1:T(2,128)}, u32[]{:S(2)}) copy-start(s32[32,2]{0,1:T(2,128)} %param.7) | copy-start | bytes 772
  433.2 69.4 %all-to-all-start = ((bf16[8,4,8192]{2,1,0:T(4,128)(2,1)}), bf16[8,4,8192]{2,1,0:T(4,128)(2,1)S(1)}, u32[]{:S(2)}, u32[]{:S(2)}) async-start(bf16[8,4,8192]{2,1,0:T(4,128)(2,1)} %stack.4), calls=%async_computation | async-start | bytes 1048576 | tf_op jit(solution)/shard_map/all_to_all | solution.py:59
  436.7 150.6 %reduce-scatter.15.cloned.1.call-start = ((), (), s32[]{:S(2)}) async-start(), calls=%async_computation.7 | async-start | bytes 4456448
  503.3 85.1 %copy-start = (f32[4,512]{1,0:T(4,128)S(1)}, f32[4,512]{1,0:T(4,128)}, u32[]{:S(2)}) copy-start(f32[4,512]{1,0:T(4,128)} %param.5) | copy-start | bytes 24580
  511.6 495.8 %reduce-scatter.17.cloned.1.call-start = ((), (), s32[]{:S(2)}) async-start(), calls=%async_computation.8 | async-start | bytes 37748736
  1011.4 69.2 %all-to-all-start.1 = ((bf16[8,4,8192]{2,1,0:T(4,128)(2,1)}), bf16[8,4,8192]{2,1,0:T(4,128)(2,1)S(1)}, u32[]{:S(2)}, u32[]{:S(2)}) async-start(bf16[8,4,8192]{2,1,0:T(4,128)(2,1)} %stack.5), calls=%async_computation.1 | async-start | bytes 1048576 | tf_op jit(solution)/shard_map/all_to_all | solution.py:59
  1014.9 150.4 %reduce-scatter.19.cloned.1.call-start = ((), (), s32[]{:S(2)}) async-start(), calls=%async_computation.9 | async-start | bytes 4456448
Sparse Core Ops, SparseCore 0:
  59.3 325.7 reduce-scatter.12
  511.7 75.5 reduce-scatter.14
  635.5 327.8 reduce-scatter.16
  1089.7 75.5 reduce-scatter.18
